TPU v7x, 32 devices: a whole 2x2x4 slice. The times are simulated.
32 devices in a mesh: fsdp: 16 (over z, y, core), seq: 2 (over x).
Axes of the slice: x: 2, y: 2, z: 4, core: 2. Of those that a mesh axis runs over, the one named last changes fastest.
Arguments:
- stream: bfloat16 [6144, 1024], P(('fsdp', 'seq')), may hold values from -6 to 6
- cotangent: bfloat16 [6144, 1024], P(('fsdp', 'seq')), may hold values from -6 to 6
- doc_lengths: int32 [10], replicated, may hold values from 1 to 1153, 6144 in all
- attention_gain: bfloat16 [1024], P('fsdp'), may hold values from 0.5 to 1.5
- query_weight: bfloat16 [1024, 1024], P('fsdp'), may hold values from -0.1875 to 0.1875
- key_matrix: bfloat16 [1024, 512], P('fsdp'), may hold values from -0.1875 to 0.1875
- value_matrix: bfloat16 [1024, 512], P('fsdp'), may hold values from -0.1875 to 0.1875
- query_gain: bfloat16 [64], P('fsdp'), may hold values from 0.5 to 1.5
- key_gain: bfloat16 [64], P('fsdp'), may hold values from 0.5 to 1.5
- output_weight: bfloat16 [1024, 1024], P('fsdp'), may hold values from -3 to 3
- feedforward_gain: bfloat16 [1024], P('fsdp'), may hold values from 0.5 to 1.5
- gate_weight: bfloat16 [1024, 4608], P('fsdp'), may hold values from -0.1875 to 0.1875
- up_weight: bfloat16 [1024, 4608], P('fsdp'), may hold values from -0.1875 to 0.1875
- down_weight: bfloat16 [4608, 1024], P('fsdp'), may hold values from -0.09375 to 0.09375
Outputs:
- result: bfloat16 [6144, 1024], P(('fsdp', 'seq'))
- grad_stream: bfloat16 [6144, 1024], P(('fsdp', 'seq'))
- grad_attention_gain: float32 [1024], P('fsdp')
- grad_query: float32 [1024, 1024], P('fsdp')
- grad_key: float32 [1024, 512], P('fsdp')
- grad_value: float32 [1024, 512], P('fsdp')
- grad_query_gain: float32 [64], P('fsdp')
- grad_key_gain: float32 [64], P('fsdp')
- grad_output: float32 [1024, 1024], P('fsdp')
- grad_feedforward_gain: float32 [1024], P('fsdp')
- grad_gate: float32 [1024, 4608], P('fsdp')
- grad_up: float32 [1024, 4608], P('fsdp')
- grad_down: float32 [4608, 1024], P('fsdp')
Inputs may be any that keep to these rules, and one draw needn't show every extreme that they name: `doc_lengths`: they sum to 6144, and the longest has exactly 1153 tokens.
All inputs are finite; a program needn't handle non-finite values.
Results may differ from a plain program's by a relative error of at most 0.03.
Values may be sent and summed in bfloat16 or wider, within the bound.
No kernel may reach another device: no remote copies, remote signals or barrier semaphores. Data moves between devices by JAX's collectives and lax.ppermute only.
A program may use at most 192 MiB of HBM per device.

v0:
```python
import math
import jax
import jax.numpy as jnp
from jax import lax
from jax.sharding import PartitionSpec as P

QUERY_HEAD_COUNT = 16
KEY_VALUE_HEADS = 8
HEAD_SIZE = 64
DOC_MIN = 1024
EPS = 1e-05
THETA = 1000000.0
NEGATIVE = -1e30


def shifted(value, axis, steps):
    count = lax.axis_size(axis)
    first, last = (max(0, -steps), min(count, count - steps))
    return lax.ppermute(value, axis, [(source, source + steps) for source in range(first, last)])


def product(left, right):
    return jnp.dot(left, right, preferred_element_type=jnp.float32)


def product_left(left, right):
    return lax.dot_general(
        left, right, (((0,), (0,)), ((), ())), preferred_element_type=jnp.float32
    )


def product_right(left, right):
    return lax.dot_general(
        left, right, (((1,), (1,)), ((), ())), preferred_element_type=jnp.float32
    )


def doc_start(starts, places):
    inside = starts[None, :] <= places[:, None]
    return jnp.max(jnp.where(inside, starts[None, :], -1), axis=1)


def rotate(values, start_offset):
    half = values.shape[-1] // 2
    ladder = jnp.arange(half, dtype=jnp.float32) * (2.0 / values.shape[-1])
    freq = jnp.power(THETA, -ladder)
    angle = start_offset.astype(jnp.float32)[:, None] * freq[None, :]
    cosine = jnp.cos(angle)[:, None, :]
    sine = jnp.sin(angle)[:, None, :]
    front = values[..., :half]
    behind = values[..., half:]
    return jnp.concatenate(
        [front * cosine - behind * sine, behind * cosine + front * sine], axis=-1
    )


def prepare_heads(linear_map, norm_gain, start_offset, heads):
    count = linear_map.shape[0]
    split = linear_map.reshape(count, heads, -1)
    normed = split * lax.rsqrt(jnp.mean(split * split, axis=-1, keepdims=True) + EPS) * norm_gain
    return rotate(normed, start_offset).reshape(count, -1)


def norm_forward(values, norm_gain):
    factor = lax.rsqrt(jnp.mean(values * values, axis=-1, keepdims=True) + EPS)
    normed = values * factor
    return (normed * norm_gain, normed, factor)


def norm_backward(grad, normed, factor, norm_gain):
    gain_grad = jnp.sum(grad * normed, axis=0)
    scaled = grad * norm_gain
    return (
        factor * (scaled - normed * jnp.mean(scaled * normed, axis=-1, keepdims=True)),
        gain_grad,
    )


def on_device(
    stream,
    cotangent,
    doc_lengths,
    attention_gain,
    query_weight,
    key_matrix,
    value_matrix,
    query_gain,
    key_gain,
    output_weight,
    feedforward_gain,
    gate_weight,
    up_weight,
    down_weight,
):
    rows = stream.shape[0]
    sequence_count = lax.axis_size("seq")
    shard_index = lax.axis_index("fsdp")
    seq_index = lax.axis_index("seq")
    block = rows * sequence_count
    lookback = max(2, -(-DOC_MIN // block))
    group_size = QUERY_HEAD_COUNT // KEY_VALUE_HEADS
    local_key_value = KEY_VALUE_HEADS // sequence_count
    scale = HEAD_SIZE ** (-0.5)
    query_row_count = math.gcd(512, block)
    blocks_q = block // query_row_count
    starts = jnp.cumsum(doc_lengths) - doc_lengths
    places = (shard_index * sequence_count + seq_index) * rows + jnp.arange(rows, dtype=jnp.int32)
    start_offset = places - doc_start(starts, places)
    query_place = shard_index * block + jnp.arange(block, dtype=jnp.int32)
    query_start = doc_start(starts, query_place)
    key_place = jnp.concatenate(
        [
            (shard_index - step) * block + jnp.arange(block, dtype=jnp.int32)
            for step in range(lookback + 1)
        ]
    )
    key_start = doc_start(starts, key_place)
    gathered = (
        lax.all_gather(attention_gain, "fsdp", axis=0, tiled=True),
        lax.all_gather(query_weight, "fsdp", axis=0, tiled=True),
        lax.all_gather(key_matrix, "fsdp", axis=0, tiled=True),
        lax.all_gather(value_matrix, "fsdp", axis=0, tiled=True),
        lax.all_gather(query_gain, "fsdp", axis=0, tiled=True),
        lax.all_gather(key_gain, "fsdp", axis=0, tiled=True),
        lax.all_gather(output_weight, "fsdp", axis=0, tiled=True),
        lax.all_gather(feedforward_gain, "fsdp", axis=0, tiled=True),
        lax.all_gather(gate_weight, "fsdp", axis=0, tiled=True),
        lax.all_gather(up_weight, "fsdp", axis=0, tiled=True),
        lax.all_gather(down_weight, "fsdp", axis=0, tiled=True),
    )
    gain_one = gathered[0].astype(jnp.float32)
    full_query = gathered[1]
    full_key = gathered[2]
    full_value = gathered[3]
    gain_query = gathered[4].astype(jnp.float32)
    gain_key = gathered[5].astype(jnp.float32)
    full_output = gathered[6]
    gain_two = gathered[7].astype(jnp.float32)
    full_gate = gathered[8]
    full_up = gathered[9]
    full_down = gathered[10]
    inputs = stream.astype(jnp.float32)
    normed_one, plain_one, factor_one = norm_forward(inputs, gain_one)
    hidden = normed_one.astype(jnp.bfloat16)
    query_lin = product(hidden, full_query)
    key_linear = product(hidden, full_key)
    value_lin = product(hidden, full_value)

    def prep_query(linear_map, norm_gain):
        return prepare_heads(linear_map, norm_gain, start_offset, QUERY_HEAD_COUNT)

    def prep_key(linear_map, norm_gain):
        return prepare_heads(linear_map, norm_gain, start_offset, KEY_VALUE_HEADS)

    query_rot, query_pull = jax.vjp(prep_query, query_lin, gain_query)
    key_rot, key_pull = jax.vjp(prep_key, key_linear, gain_key)
    query_heads, key_heads, value_heads = (
        lax.all_to_all(
            query_rot.astype(jnp.bfloat16), "seq", split_axis=1, concat_axis=0, tiled=True
        ),
        lax.all_to_all(
            key_rot.astype(jnp.bfloat16), "seq", split_axis=1, concat_axis=0, tiled=True
        ),
        lax.all_to_all(
            value_lin.astype(jnp.bfloat16), "seq", split_axis=1, concat_axis=0, tiled=True
        ),
    )
    key_pair = jnp.stack([key_heads, value_heads])
    pairs = [key_pair]
    moving = key_pair
    for step in range(lookback):
        moving = shifted(moving, "fsdp", 1)
        pairs.append(moving)
    all_keys = jnp.concatenate([pair[0] for pair in pairs]).reshape(-1, local_key_value, HEAD_SIZE)
    all_values = jnp.concatenate([pair[1] for pair in pairs]).reshape(
        -1, local_key_value, HEAD_SIZE
    )
    query_split = query_heads.reshape(
        blocks_q, query_row_count, local_key_value, group_size, HEAD_SIZE
    )
    start_split = query_start.reshape(blocks_q, query_row_count)
    place_split = query_place.reshape(blocks_q, query_row_count)

    def scores_of(query_tile, start_block, place_block):
        score = (
            jnp.einsum("qhgd,khd->hgqk", query_tile, all_keys, preferred_element_type=jnp.float32)
            * scale
        )
        allowed = (key_start[None, :] == start_block[:, None]) & (
            key_place[None, :] <= place_block[:, None]
        )
        return jnp.where(allowed, score, NEGATIVE)

    def attend(items):
        query_tile, start_block, place_block = items
        score = scores_of(query_tile, start_block, place_block)
        highest = jnp.max(score, axis=-1, keepdims=True)
        weight = jnp.exp(score - highest)
        total = jnp.sum(weight, axis=-1, keepdims=True)
        mixed = jnp.einsum(
            "hgqk,khd->qhgd",
            (weight / total).astype(jnp.bfloat16),
            all_values,
            preferred_element_type=jnp.float32,
        )
        return (
            mixed.reshape(query_row_count, -1).astype(jnp.bfloat16),
            (highest + jnp.log(total))[..., 0],
        )

    mixed_heads, log_total = lax.map(attend, (query_split, start_split, place_split))
    attended = lax.all_to_all(
        mixed_heads.reshape(block, -1), "seq", split_axis=0, concat_axis=1, tiled=True
    )
    middle = inputs + product(attended, full_output)
    normed_two, plain_two, factor_two = norm_forward(middle, gain_two)
    hidden_two = normed_two.astype(jnp.bfloat16)
    gate = product(hidden_two, full_gate)
    upward = product(hidden_two, full_up)
    inner = (jax.nn.silu(gate) * upward).astype(jnp.bfloat16)
    result = (middle + product(inner, full_down)).astype(jnp.bfloat16)
    d_inner = product_right(cotangent, full_down)
    sigma = jax.nn.sigmoid(gate)
    d_gate = (d_inner * upward * sigma * (1.0 + gate * (1.0 - sigma))).astype(jnp.bfloat16)
    d_up = (d_inner * gate * sigma).astype(jnp.bfloat16)
    d_two = product_right(d_gate, full_gate) + product_right(d_up, full_up)
    d_norm_two, grad_gain_two = norm_backward(d_two, plain_two, factor_two, gain_two)
    d_middle = cotangent.astype(jnp.float32) + d_norm_two
    d_mid = d_middle.astype(jnp.bfloat16)
    d_attended = product_right(d_mid, full_output).astype(jnp.bfloat16)
    d_heads = lax.all_to_all(d_attended, "seq", split_axis=1, concat_axis=0, tiled=True)
    d_split = d_heads.reshape(blocks_q, query_row_count, local_key_value, group_size, HEAD_SIZE)

    def attend_back(carry, items):
        d_keys, d_values = carry
        query_tile, start_block, place_block, d_block, total_block = items
        score = scores_of(query_tile, start_block, place_block)
        prob = jnp.exp(score - total_block[..., None])
        d_prob = jnp.einsum(
            "qhgd,khd->hgqk", d_block, all_values, preferred_element_type=jnp.float32
        )
        row_sum = jnp.sum(prob * d_prob, axis=-1, keepdims=True)
        d_score = (prob * (d_prob - row_sum)).astype(jnp.bfloat16)
        d_query = (
            jnp.einsum("hgqk,khd->qhgd", d_score, all_keys, preferred_element_type=jnp.float32)
            * scale
        )
        d_keys = (
            d_keys
            + jnp.einsum("hgqk,qhgd->khd", d_score, query_tile, preferred_element_type=jnp.float32)
            * scale
        )
        d_values = d_values + jnp.einsum(
            "hgqk,qhgd->khd", prob.astype(jnp.bfloat16), d_block, preferred_element_type=jnp.float32
        )
        return ((d_keys, d_values), d_query.reshape(query_row_count, -1).astype(jnp.bfloat16))

    empty = jnp.zeros(all_keys.shape, jnp.float32)
    (d_keys, d_values), d_queries = lax.scan(
        attend_back, (empty, empty), (query_split, start_split, place_split, d_split, log_total)
    )
    key_parts = d_keys.reshape(lookback + 1, block, local_key_value * HEAD_SIZE)
    value_parts = d_values.reshape(lookback + 1, block, local_key_value * HEAD_SIZE)
    parts = [jnp.stack([key_parts[step], value_parts[step]]) for step in range(lookback + 1)]
    d_pair = parts[lookback]
    for step in range(lookback, 0, -1):
        d_pair = (
            shifted(d_pair.astype(jnp.bfloat16), "fsdp", -1).astype(d_pair.dtype) + parts[step - 1]
        )
    d_query_tok, d_key_tok, d_value_tok = (
        lax.all_to_all(
            d_queries.reshape(block, -1), "seq", split_axis=0, concat_axis=1, tiled=True
        ),
        lax.all_to_all(
            d_pair[0].astype(jnp.bfloat16), "seq", split_axis=0, concat_axis=1, tiled=True
        ),
        lax.all_to_all(
            d_pair[1].astype(jnp.bfloat16), "seq", split_axis=0, concat_axis=1, tiled=True
        ),
    )
    d_query_lin, grad_query_gain = query_pull(d_query_tok.astype(jnp.float32))
    d_key_lin, grad_key_gain = key_pull(d_key_tok.astype(jnp.float32))
    d_query_low = d_query_lin.astype(jnp.bfloat16)
    d_key_low = d_key_lin.astype(jnp.bfloat16)
    d_hidden = (
        product_right(d_query_low, full_query)
        + product_right(d_key_low, full_key)
        + product_right(d_value_tok, full_value)
    )
    d_norm_one, grad_gain_one = norm_backward(d_hidden, plain_one, factor_one, gain_one)
    grad_stream = (d_middle + d_norm_one).astype(jnp.bfloat16)
    grad_down = product_left(inner, cotangent)
    grad_gate = product_left(hidden_two, d_gate)
    grad_up = product_left(hidden_two, d_up)
    grad_output = product_left(attended, d_mid)
    grad_query = product_left(hidden, d_query_low)
    grad_key = product_left(hidden, d_key_low)
    grad_value = product_left(hidden, d_value_tok)
    shards = (
        lax.psum_scatter(
            grad_gain_one.astype(jnp.bfloat16), "fsdp", scatter_dimension=0, tiled=True
        ).astype(jnp.float32),
        lax.psum_scatter(
            grad_query.astype(jnp.bfloat16), "fsdp", scatter_dimension=0, tiled=True
        ).astype(jnp.float32),
        lax.psum_scatter(
            grad_key.astype(jnp.bfloat16), "fsdp", scatter_dimension=0, tiled=True
        ).astype(jnp.float32),
        lax.psum_scatter(
            grad_value.astype(jnp.bfloat16), "fsdp", scatter_dimension=0, tiled=True
        ).astype(jnp.float32),
        lax.psum_scatter(
            grad_query_gain.astype(jnp.bfloat16), "fsdp", scatter_dimension=0, tiled=True
        ).astype(jnp.float32),
        lax.psum_scatter(
            grad_key_gain.astype(jnp.bfloat16), "fsdp", scatter_dimension=0, tiled=True
        ).astype(jnp.float32),
        lax.psum_scatter(
            grad_output.astype(jnp.bfloat16), "fsdp", scatter_dimension=0, tiled=True
        ).astype(jnp.float32),
        lax.psum_scatter(
            grad_gain_two.astype(jnp.bfloat16), "fsdp", scatter_dimension=0, tiled=True
        ).astype(jnp.float32),
        lax.psum_scatter(
            grad_gate.astype(jnp.bfloat16), "fsdp", scatter_dimension=0, tiled=True
        ).astype(jnp.float32),
        lax.psum_scatter(
            grad_up.astype(jnp.bfloat16), "fsdp", scatter_dimension=0, tiled=True
        ).astype(jnp.float32),
        lax.psum_scatter(
            grad_down.astype(jnp.bfloat16), "fsdp", scatter_dimension=0, tiled=True
        ).astype(jnp.float32),
    )
    totals = (
        lax.psum(shards[0].astype(jnp.bfloat16), "seq").astype(jnp.float32),
        lax.psum(shards[1].astype(jnp.bfloat16), "seq").astype(jnp.float32),
        lax.psum(shards[2].astype(jnp.bfloat16), "seq").astype(jnp.float32),
        lax.psum(shards[3].astype(jnp.bfloat16), "seq").astype(jnp.float32),
        lax.psum(shards[4].astype(jnp.bfloat16), "seq").astype(jnp.float32),
        lax.psum(shards[5].astype(jnp.bfloat16), "seq").astype(jnp.float32),
        lax.psum(shards[6].astype(jnp.bfloat16), "seq").astype(jnp.float32),
        lax.psum(shards[7].astype(jnp.bfloat16), "seq").astype(jnp.float32),
        lax.psum(shards[8].astype(jnp.bfloat16), "seq").astype(jnp.float32),
        lax.psum(shards[9].astype(jnp.bfloat16), "seq").astype(jnp.float32),
        lax.psum(shards[10].astype(jnp.bfloat16), "seq").astype(jnp.float32),
    )
    outputs = (
        totals[0],
        totals[1],
        totals[2],
        totals[3],
        totals[4],
        totals[5],
        totals[6],
        totals[7],
        totals[8],
        totals[9],
        totals[10],
    )
    return (result, grad_stream) + outputs


def solution(mesh):
    placed = (
        P(("fsdp", "seq"), None),
        P(("fsdp", "seq"), None),
        P(),
        P("fsdp"),
        P("fsdp", None),
        P("fsdp", None),
        P("fsdp", None),
        P("fsdp"),
        P("fsdp"),
        P("fsdp", None),
        P("fsdp"),
        P("fsdp", None),
        P("fsdp", None),
        P("fsdp", None),
    )
    return jax.shard_map(
        on_device,
        mesh=mesh,
        in_specs=placed,
        out_specs=(
            P(("fsdp", "seq"), None),
            P(("fsdp", "seq"), None),
            P("fsdp"),
            P("fsdp", None),
            P("fsdp", None),
            P("fsdp", None),
            P("fsdp"),
            P("fsdp"),
            P("fsdp", None),
            P("fsdp"),
            P("fsdp", None),
            P("fsdp", None),
            P("fsdp", None),
        ),
        check_vma=False,
    )
```

profile of v0, /device:TPU:0, one launch (start us, length us, event | category | flops | bytes accessed | tf_op | source)
XLA Modules:
  0.0 1242.6 jit_solution(9412781983288827578)
XLA Ops:
  17.9 36.1 %all-reduce.13 = (bf16[64]{0:T(256)(128)(2,1)S(1)}, bf16[1024]{0:T(1024)(128)(2,1)S(1)}, bf16[64]{0:T(256)(128)(2,1)S(1)}, bf16[1024]{0:T(1024)(128)(2,1)}) all-reduce(bf16[64]{0:T(256)(128)(2,1)S(1)} %dynamic-update-slice.1, bf16[1024]{0:T(1024)(128)(2,1)S(1)} %dynamic-update-slice, ...), channel_id=1, replica_groups=mesh['fsdp'=16,'seq'=2] {'fsdp'}, use_global_device_ids=true, to_apply=%add.5 | all-reduce | flops 2176 | bytes 8704
  63.0 27.1 %all-gather.10.cloned.1.call-done = bf16[1024,512]{1,0:T(8,128)(2,1)} async-done(((bf16[64,512]{1,0:T(8,128)(2,1)}), bf16[1024,512]{1,0:T(8,128)(2,1)}) %all-gather.10.cloned.1.call-update) | async-done | bytes 1048592 | tf_op jit(solution)/shard_map/all_gather | solution.py:121
  93.2 7.6 all_to_all.116
  112.0 9.3 collective-permute-start.2
  123.5 10.6 all-gather.8.cloned.1.call-done
  151.9 27.9 %while.27 = (s32[]{:T(128)}, bf16[3,128,512]{2,1,0:T(8,128)(2,1)}, f32[3,4,2,128]{3,2,1,0:T(2,128)}, s32[1536]{0:T(1024)S(1)}, s32[3,128]{1,0:T(4,128)}, /*index...) while((s32[]{:T(128)}, bf16[3,128,512]{2,1,0:T(8,128)(2,1)}, ...), condition=%wide.region_10.11_spmd, body=%wide.region_7.10_spmd.sunk | while | flops 422181888 | bytes 22068356 | solution.py:211
  192.9 65.6 %all-gather.16.cloned.1.call-done = bf16[1024,4608]{1,0:T(8,128)(2,1)} async-done(((bf16[64,4608]{1,0:T(8,128)(2,1)}), bf16[1024,4608]{1,0:T(8,128)(2,1)}) %all-gather.16.cloned.1.call-update) | async-done | bytes 9437200 | tf_op jit(solution)/shard_map/all_gather | solution.py:127
  258.5 7.5 fusion.85
  266.0 74.3 %all-gather.18.cloned.1.call-done = bf16[1024,4608]{1,0:T(8,128)(2,1)} async-done(((bf16[64,4608]{1,0:T(8,128)(2,1)}), bf16[1024,4608]{1,0:T(8,128)(2,1)}) %all-gather.18.cloned.1.call-update) | async-done | bytes 9437200 | tf_op jit(solution)/shard_map/all_gather | solution.py:128
  340.3 7.5 fusion.86
  347.7 74.4 %all-gather.20.cloned.1.call-done = bf16[4608,1024]{1,0:T(8,128)(2,1)} async-done(((bf16[288,1024]{1,0:T(8,128)(2,1)}), bf16[4608,1024]{1,0:T(8,128)(2,1)}) %all-gather.20.cloned.1.call-update) | async-done | bytes 9437200 | tf_op jit(solution)/shard_map/all_gather | solution.py:129
  422.2 11.2 multiply_convert_fusion
  433.4 8.2 fusion.87
  452.4 7.0 all-to-all-done.4
  462.3 63.8 %while.28 = (s32[]{:T(128)}, f32[1536,4,64]{0,2,1:T(8,128)}, f32[1536,4,64]{0,2,1:T(8,128)}, bf16[3,128,512]{2,1,0:T(8,128)(2,1)}, bf16[3,128,4,2,64]{1,4,3,2,0:...) while((s32[]{:T(128)}, f32[1536,4,64]{0,2,1:T(8,128)}, ...), condition=%wide.region_15.16_spmd.clone, body=%wide.region_13.15_spmd.clone.sunk | while | flops 1023474688 | bytes 107777264 | solution.py:259
  533.3 6.7 collective-permute-done.4
  541.6 7.8 collective-permute-done.5
  549.7 7.2 all_to_all.117
  560.0 7.2 all_to_all.118
  571.1 8.4 all_to_all.119
  587.0 6.6 convolution_convert_fusion.2
  601.2 6.7 convolution_convert_fusion
  609.4 12.3 reduce-scatter.10.cloned.1.call-done
  621.7 61.1 %reduce-scatter.12.cloned.1.call-done = bf16[64,512]{1,0:T(8,128)(2,1)} async-done(((bf16[1024,512]{1,0:T(8,128)(2,1)}), bf16[64,512]{1,0:T(8,128)(2,1)}) %reduce-scatter.12.cloned.1.call-update) | async-done | bytes 65552 | tf_op jit(solution)/shard_map/reduce_scatter | solution.py:309
  682.8 64.1 %reduce-scatter.14.cloned.1.call-done = bf16[64,1024]{1,0:T(8,128)(2,1)} async-done(((bf16[1024,1024]{1,0:T(8,128)(2,1)}), bf16[64,1024]{1,0:T(8,128)(2,1)}) %reduce-scatter.14.cloned.1.call-update) | async-done | bytes 131088 | tf_op jit(solution)/shard_map/reduce_scatter | solution.py:318
  746.9 64.8 %reduce-scatter.8.cloned.1.call-done = bf16[64,1024]{1,0:T(8,128)(2,1)} async-done(((bf16[1024,1024]{1,0:T(8,128)(2,1)}), bf16[64,1024]{1,0:T(8,128)(2,1)}) %reduce-scatter.8.cloned.1.call-update) | async-done | bytes 131088 | tf_op jit(solution)/shard_map/reduce_scatter | solution.py:303
  811.7 114.3 %reduce-scatter.16.cloned.1.call-done = bf16[64,4608]{1,0:T(8,128)(2,1)} async-done(((bf16[1024,4608]{1,0:T(8,128)(2,1)}), bf16[64,4608]{1,0:T(8,128)(2,1)}) %reduce-scatter.16.cloned.1.call-update) | async-done | bytes 589840 | tf_op jit(solution)/shard_map/reduce_scatter | solution.py:324
  926.1 115.8 %reduce-scatter.18.cloned.1.call-done = bf16[64,4608]{1,0:T(8,128)(2,1)} async-done(((bf16[1024,4608]{1,0:T(8,128)(2,1)}), bf16[64,4608]{1,0:T(8,128)(2,1)}) %reduce-scatter.18.cloned.1.call-update) | async-done | bytes 589840 | tf_op jit(solution)/shard_map/reduce_scatter | solution.py:327
  1041.9 115.1 %reduce-scatter.20.cloned.1.call-done = bf16[288,1024]{1,0:T(8,128)(2,1)} async-done(((bf16[4608,1024]{1,0:T(8,128)(2,1)}), bf16[288,1024]{1,0:T(8,128)(2,1)}) %reduce-scatter.20.cloned.1.call-update) | async-done | bytes 589840 | tf_op jit(solution)/shard_map/reduce_scatter | solution.py:330
  1157.0 7.1 fusion.48
  1166.9 32.4 %all-reduce.12 = (bf16[1024]{0:T(1024)(128)(2,1)S(1)}, bf16[64]{0:T(256)(128)(2,1)S(1)}, bf16[64]{0:T(256)(128)(2,1)S(1)}, bf16[1024]{0:T(1024)(128)(2,1)S(1)}) all-reduce(bf16[1024]{0:T(1024)(128)(2,1)S(1)} %get-tuple-element.276, bf16[64]{0:T(256)(128)(2,1)S(1)} %get-tuple-element.278, ...), channel_id=2, replica_groups=mesh['fsdp'=16,'seq'=2] {'fsdp'}, use_global_device_ids=true, to_apply=%region_20.21.clone | all-reduce | flops 2176 | bytes 8704
  1207.6 17.5 %all-reduce.18.cloned.1.call-done = (bf16[64,1024]{1,0:T(8,128)(2,1)}, bf16[64,512]{1,0:T(8,128)(2,1)}, bf16[64,512]{1,0:T(8,128)(2,1)}, bf16[64,1024]{1,0:T(8,1...) async-done(((bf16[64,1024]{1,0:T(8,128)(2,1)}, bf16[64,512]{1,0:T(8,128)(2,1)}, bf16[64,512]{1,0:T(8,128)(2,1)}, ...) | async-done | bytes 2162704 | tf_op jit(solution)/shard_map/psum | solution.py:336
  (350 shorter events, 222.9 us)
Async XLA Ops:
  7.2 83.0 %copy-start.6 = (bf16[192,1024]{1,0:T(8,128)(2,1)S(1)}, bf16[192,1024]{1,0:T(8,128)(2,1)}, u32[]{:S(2)}) copy-start(bf16[192,1024]{1,0:T(8,128)(2,1)} %param.18) | copy-start | bytes 1179652
  7.2 49.9 %all-gather.12.cloned.1.call-start = ((), (), s32[]{:S(2)}) async-start(), calls=%async_computation.17 | async-start | bytes 1114112 | tf_op jit(solution)/shard_map/all_gather | solution.py:122
  7.9 82.2 %all-gather.10.cloned.1.call-start = ((), (), s32[]{:S(2)}) async-start(), calls=%async_computation.16 | async-start | bytes 1114112 | tf_op jit(solution)/shard_map/all_gather | solution.py:121
  8.7 125.4 %all-gather.8.cloned.1.call-start = ((), (), s32[]{:S(2)}) async-start(), calls=%async_computation.15 | async-start | bytes 2228224 | tf_op jit(solution)/shard_map/all_gather | solution.py:120
  9.4 180.9 %all-gather.14.cloned.1.call-start = ((), (), s32[]{:S(2)}) async-start(), calls=%async_computation.18 | async-start | bytes 2228224 | tf_op jit(solution)/shard_map/all_gather | solution.py:125
  10.0 248.5 %all-gather.16.cloned.1.call-start = ((), (), s32[]{:S(2)}) async-start(), calls=%async_computation.19 | async-start | bytes 10027008 | tf_op jit(solution)/shard_map/all_gather | solution.py:127
  10.6 329.7 %all-gather.18.cloned.1.call-start = ((), (), s32[]{:S(2)}) async-start(), calls=%async_computation.20 | async-start | bytes 10027008 | tf_op jit(solution)/shard_map/all_gather | solution.py:128
  11.1 411.0 %all-gather.20.cloned.1.call-start = ((), (), s32[]{:S(2)}) async-start(), calls=%async_computation.21 | async-start | bytes 10027008 | tf_op jit(solution)/shard_map/all_gather | solution.py:129
  54.0 80.1 %copy-start.39 = (f32[1024]{0:T(1024)}, f32[1024]{0:T(1024)S(1)}, u32[]{:S(2)}) copy-start(f32[1024]{0:T(1024)S(1)} %convert_element_type.254) | copy-start | bytes 12292
  57.0 80.8 %copy-start.27 = (f32[192,32]{0,1:T(8,128)}, f32[192,32]{0,1:T(8,128)S(1)}, u32[]{:S(2)}) copy-start(f32[192,32]{0,1:T(8,128)S(1)} %get-tuple-element.380) | copy-start | bytes 73732
  57.1 80.8 %copy-start.29 = (f32[192,32]{0,1:T(8,128)}, f32[192,32]{0,1:T(8,128)S(1)}, u32[]{:S(2)}) copy-start(f32[192,32]{0,1:T(8,128)S(1)} %get-tuple-element.381) | copy-start | bytes 73732
  59.6 33.6 %all-to-all-start.2 = ((bf16[192,2,256]{2,0,1:T(8,128)(2,1)}), bf16[192,2,256]{2,0,1:T(8,128)(2,1)S(1)}, u32[]{:S(2)}, u32[]{:S(2)}) async-start(bf16[192,2,256]{2,0,1:T(8,128)(2,1)} %bitcast.212), calls=%async_computation.2 | async-start | bytes 393216 | tf_op jit(solution)/shard_map/all_to_all | solution.py:164
  100.8 2.6 collective-permute-start
  103.4 8.6 collective-permute-start.1
  112.0 10.0 collective-permute-start.2
  139.1 11.0 all-to-all-start
  179.8 10.4 all-to-all-start.3
  192.8 252.7 %copy-start.10 = (f32[192,1024]{1,0:T(8,128)}, f32[192,1024]{1,0:T(8,128)S(1)}, u32[]{:S(2)}) copy-start(f32[192,1024]{1,0:T(8,128)S(1)} %get-tuple-element.389) | copy-start | bytes 2359300
  192.9 147.3 %copy-start.8 = (bf16[192,1024]{1,0:T(8,128)(2,1)}, bf16[192,1024]{1,0:T(8,128)(2,1)S(1)}, u32[]{:S(2)}) copy-start(bf16[192,1024]{1,0:T(8,128)(2,1)S(1)} %multiply_convert_fusion.3) | copy-start | bytes 1179652
  448.7 10.7 all-to-all-start.4
  452.2 169.5 %reduce-scatter.10.cloned.1.call-start = ((), (), s32[]{:S(2)}) async-start(), calls=%async_computation.23 | async-start | bytes 1114112 | tf_op jit(solution)/shard_map/reduce_scatter | solution.py:306
  528.3 3.6 collective-permute-start.3
  532.0 8.0 collective-permute-start.4
  540.2 9.2 collective-permute-start.5
  559.8 123.0 %reduce-scatter.12.cloned.1.call-start = ((), (), s32[]{:S(2)}) async-start(), calls=%async_computation.24 | async-start | bytes 1114112 | tf_op jit(solution)/shard_map/reduce_scatter | solution.py:309
  568.8 178.1 %reduce-scatter.14.cloned.1.call-start = ((), (), s32[]{:S(2)}) async-start(), calls=%async_computation.25 | async-start | bytes 2228224 | tf_op jit(solution)/shard_map/reduce_scatter | solution.py:318
  571.0 240.7 %reduce-scatter.8.cloned.1.call-start = ((), (), s32[]{:S(2)}) async-start(), calls=%async_computation.22 | async-start | bytes 2228224 | tf_op jit(solution)/shard_map/reduce_scatter | solution.py:303
  586.7 339.3 %reduce-scatter.16.cloned.1.call-start = ((), (), s32[]{:S(2)}) async-start(), calls=%async_computation.26 | async-start | bytes 10027008 | tf_op jit(solution)/shard_map/reduce_scatter | solution.py:324
  593.6 448.2 %reduce-scatter.18.cloned.1.call-start = ((), (), s32[]{:S(2)}) async-start(), calls=%async_computation.27 | async-start | bytes 10027008 | tf_op jit(solution)/shard_map/reduce_scatter | solution.py:327
  600.3 556.7 %reduce-scatter.20.cloned.1.call-start = ((), (), s32[]{:S(2)}) async-start(), calls=%async_computation.28 | async-start | bytes 10027008 | tf_op jit(solution)/shard_map/reduce_scatter | solution.py:330
  608.0 549.0 %copy-start.11 = (f32[192,1024]{1,0:T(8,128)S(1)}, f32[192,1024]{1,0:T(8,128)}, u32[]{:S(2)}) copy-start(f32[192,1024]{1,0:T(8,128)} %copy-done.10) | copy-start | bytes 2359300
  608.0 617.1 %all-reduce.18.cloned.1.call-start = ((), (), s32[]{:S(2)}) async-start(), calls=%async_computation.29 | async-start | bytes 4325376 | tf_op jit(solution)/shard_map/psum | solution.py:336
  (53 other events, 557.9 us)
Sparse Core Ops, SparseCore 0:
  10.2 40.8 all-gather.11
  53.2 36.8 all-gather.9
  92.3 41.7 all-gather.7
  136.1 39.9 all-gather.13
  178.3 80.2 all-gather.15
  260.7 79.5 all-gather.17
  342.5 79.5 all-gather.19
  559.9 61.7 reduce-scatter.9
  626.3 56.4 reduce-scatter.11
  686.4 60.5 reduce-scatter.13
  751.1 60.5 reduce-scatter.7
  815.7 110.3 reduce-scatter.15
  930.7 111.1 reduce-scatter.17
  1045.8 111.1 reduce-scatter.19
  1159.8 65.2 all-reduce.17
where the time goes:
time: 1250 us; the launch traced here: 1240 us
  waiting for transfers between devices  858 us (69%)
  matrix products  145 us (12%)
  blocking collectives  104 us (8%)
  local copies, waits for them, and re-layouts  46.4 us (4%)
  starting transfers between devices  36.8 us (3%)
  other arithmetic  35.1 us (3%)
  between operations  18 us (1%)
    reduce_scatter x1, waiting for transfers between devices, on_device(): lax.psum_scatter(grad_up.astype(jnp.bfloat16), 'fsdp', scatter_dimension=...  116 us
    reduce_scatter x1, waiting for transfers between devices, on_device(): lax.psum_scatter(grad_down.astype(jnp.bfloat16), 'fsdp', scatter_dimensio...  115 us
    reduce_scatter x1, waiting for transfers between devices, on_device(): lax.psum_scatter(grad_gate.astype(jnp.bfloat16), 'fsdp', scatter_dimensio...  114 us
    all_gather x1, waiting for transfers between devices, on_device(): lax.all_gather(down_weight, 'fsdp', axis=0, tiled=True)  74.4 us
    all_gather x1, waiting for transfers between devices, on_device(): lax.all_gather(up_weight, 'fsdp', axis=0, tiled=True)  74.3 us
    unnamed x2, blocking collectives  68.5 us
    all_gather x1, waiting for transfers between devices, on_device(): lax.all_gather(gate_weight, 'fsdp', axis=0, tiled=True)  65.6 us
    reduce_scatter x1, waiting for transfers between devices, on_device(): lax.psum_scatter(grad_query.astype(jnp.bfloat16), 'fsdp', scatter_dimensi...  64.8 us
  transfers between devices with their start and end apart: 25, of which 20 were waited for; matrix products, arithmetic and copies ran while one was open for 9% of the time, Pallas kernels for 0%

commit v1 on v0

--- a/solution.py
+++ b/solution.py
@@ -11,6 +11,24 @@
 EPS = 1e-05
 THETA = 1000000.0
 NEGATIVE = -1e30
+
+
+def gather_around(array, axis, dim):
+    ways, here, step = (lax.axis_size(axis), lax.axis_index(axis), array.shape[dim])
+    dims = [n * ways if d == dim else n for d, n in enumerate(array.shape)]
+    full = lax.dynamic_update_slice_in_dim(
+        jnp.zeros(dims, array.dtype), array, here * step, axis=dim
+    )
+    going_up = going_down = array
+    for far in range(1, ways // 2 + 1):
+        going_up = lax.ppermute(going_up, axis, [(d, (d + 1) % ways) for d in range(ways)])
+        full = lax.dynamic_update_slice_in_dim(full, going_up, (here - far) % ways * step, axis=dim)
+        if 2 * far < ways:
+            going_down = lax.ppermute(going_down, axis, [(d, (d - 1) % ways) for d in range(ways)])
+            full = lax.dynamic_update_slice_in_dim(
+                full, going_down, (here + far) % ways * step, axis=dim
+            )
+    return full
 
 
 def shifted(value, axis, steps):
@@ -126,7 +144,7 @@
         lax.all_gather(feedforward_gain, "fsdp", axis=0, tiled=True),
         lax.all_gather(gate_weight, "fsdp", axis=0, tiled=True),
         lax.all_gather(up_weight, "fsdp", axis=0, tiled=True),
-        lax.all_gather(down_weight, "fsdp", axis=0, tiled=True),
+        gather_around(down_weight, "fsdp", 0),
     )
     gain_one = gathered[0].astype(jnp.float32)
     full_query = gathered[1]

time: 1250 us -> 1210 us (0.968)
  waiting for transfers between devices: 858 us -> 749 us
  starting transfers between devices: 36.8 us -> 85.7 us
  local copies, waits for them, and re-layouts: 46.4 us -> 74.9 us
    all_gather x1 -> x0, waiting for transfers between devices: 74.4 us -> none  [on_device(): lax.all_gather(down_weight, 'fsdp', axis=0, tiled=True)]
    ppermute x0 -> x15, starting transfers between devices: none -> 38.9 us  [the longest x8 20.3 us: gather_around(): lax.ppermute(going_up, axis, [(d, (d + 1) % ways) for d in range(ways)])]
    all_gather x1, waiting for transfers between devices: 27.1 us -> 0.01 us  [on_device(): lax.all_gather(key_matrix, 'fsdp', axis=0, tiled=True)]
    dynamic_update_slice x0 -> x16, local copies, waits for them, and re-layouts: none -> 26.9 us  [the longest x8 13.5 us: gather_around(): lax.dynamic_update_slice_in_dim(full, going_up, (here - far) % ways * ste...]
  transfers between devices with their start and end apart: 25 -> 40, of which waited for: 20 -> 18; matrix products, arithmetic and copies ran while one was open for 9% -> 11% of each run, Pallas kernels for 0% -> 0%
where the time goes in v1:
time: 1210 us; the launch traced here: 1200 us
  waiting for transfers between devices  749 us (62%)
  matrix products  135 us (11%)
  blocking collectives  99.7 us (8%)
  starting transfers between devices  85.7 us (7%)
  local copies, waits for them, and re-layouts  74.9 us (6%)
  other arithmetic  32.1 us (3%)
  between operations  18 us (1%)
    reduce_scatter x1, waiting for transfers between devices, on_device(): lax.psum_scatter(grad_up.astype(jnp.bfloat16), 'fsdp', scatter_dimension=...  116 us
    reduce_scatter x1, waiting for transfers between devices, on_device(): lax.psum_scatter(grad_down.astype(jnp.bfloat16), 'fsdp', scatter_dimensio...  115 us
    reduce_scatter x1, waiting for transfers between devices, on_device(): lax.psum_scatter(grad_gate.astype(jnp.bfloat16), 'fsdp', scatter_dimensio...  114 us
    all_gather x1, waiting for transfers between devices, on_device(): lax.all_gather(up_weight, 'fsdp', axis=0, tiled=True)  74.2 us
    unnamed x2, blocking collectives  71.9 us
    reduce_scatter x1, waiting for transfers between devices, on_device(): lax.psum_scatter(grad_query.astype(jnp.bfloat16), 'fsdp', scatter_dimensi...  64.7 us
    all_gather x1, waiting for transfers between devices, on_device(): lax.all_gather(gate_weight, 'fsdp', axis=0, tiled=True)  64.5 us
    reduce_scatter x1, waiting for transfers between devices, on_device(): lax.psum_scatter(grad_output.astype(jnp.bfloat16), 'fsdp', scatter_dimens...  64.3 us
  transfers between devices with their start and end apart: 40, of which 18 were waited for; matrix products, arithmetic and copies ran while one was open for 11% of the time, Pallas kernels for 0%

profile of v1, /device:TPU:0, one launch (start us, length us, event | category | flops | bytes accessed | tf_op | source)
XLA Modules:
  0.0 1195.4 jit_solution(14154277808477352932)
XLA Ops:
  32.6 39.3 %all-reduce.13 = (bf16[64]{0:T(256)(128)(2,1)S(1)}, bf16[1024]{0:T(1024)(128)(2,1)S(1)}, bf16[64]{0:T(256)(128)(2,1)S(1)}, bf16[1024]{0:T(1024)(128)(2,1)S(1)}) all-reduce(bf16[64]{0:T(256)(128)(2,1)S(1)} %dynamic-update-slice.1, bf16[1024]{0:T(1024)(128)(2,1)S(1)} %dynamic-update-slice, ...), channel_id=1, replica_groups=mesh['fsdp'=16,'seq'=2] {'fsdp'}, use_global_device_ids=true, to_apply=%add.5 | all-reduce | flops 2176 | bytes 8704
  85.1 12.3 %all-gather.11.cloned.1.call-done = bf16[1024,512]{1,0:T(8,128)(2,1)} async-done(((bf16[64,512]{1,0:T(8,128)(2,1)}), bf16[1024,512]{1,0:T(8,128)(2,1)}) %all-gather.11.cloned.1.call-update) | async-done | bytes 1048592 | tf_op jit(solution)/shard_map/all_gather | solution.py:140
  123.0 11.1 collective-permute-start.1
  138.4 11.9 collective-permute-start.2
  163.1 8.4 collective-permute-start.15
  188.4 21.2 %while.27 = (s32[]{:T(128)}, bf16[3,128,512]{2,1,0:T(8,128)(2,1)}, f32[3,4,2,128]{3,2,1,0:T(2,128)}, s32[1536]{0:T(1024)S(1)}, s32[3,128]{1,0:T(4,128)}, /*index...) while((s32[]{:T(128)}, bf16[3,128,512]{2,1,0:T(8,128)(2,1)}, ...), condition=%wide.region_10.11_spmd, body=%wide.region_7.10_spmd.sunk | while | flops 422181888 | bytes 22069364 | solution.py:229
  226.0 64.5 %all-gather.15.cloned.1.call-done = bf16[1024,4608]{1,0:T(8,128)(2,1)} async-done(((bf16[64,4608]{1,0:T(8,128)(2,1)}), bf16[1024,4608]{1,0:T(8,128)(2,1)}) %all-gather.15.cloned.1.call-update) | async-done | bytes 9437200 | tf_op jit(solution)/shard_map/all_gather | solution.py:145
  290.5 7.5 fusion.85
  298.1 74.2 %all-gather.17.cloned.1.call-done = bf16[1024,4608]{1,0:T(8,128)(2,1)} async-done(((bf16[64,4608]{1,0:T(8,128)(2,1)}), bf16[1024,4608]{1,0:T(8,128)(2,1)}) %all-gather.17.cloned.1.call-update) | async-done | bytes 9437200 | tf_op jit(solution)/shard_map/all_gather | solution.py:146
  372.3 7.6 fusion.86
  380.0 12.8 %multiply_convert_fusion = (bf16[192,4608]{1,0:T(8,128)(2,1)}, bf16[192,4608]{1,0:T(8,128)(2,1)}, bf16[192,4608]{1,0:T(8,128)(2,1)}) fusion(f32[192,4608]{1,0:T(8,128)S(1)} %copy-done.23, f32[192,4608]{1,0:T(8,128)} %fusion.86, bf16[4608,1024]{1,0:T(8,128)(2,1)} %constant_dynamic-update-slice_fusion.2, bf16[192,1024]{1,0:T(8,128)(2,1)S(1)} %copy-done.28), kind=kOutput, calls=%fused_computation.67 | convolution fusion | flops 1826095104 | bytes 22216704 | tf_op jit(solution)/shard_map/dot_general | solution.py:51
  397.6 5.4 multiply_reduce_fusion.3
  409.7 6.8 all-to-all-done.4
  418.3 62.3 %while.28 = (s32[]{:T(128)}, f32[1536,4,64]{0,2,1:T(8,128)}, f32[1536,4,64]{0,2,1:T(8,128)}, bf16[3,128,512]{2,1,0:T(8,128)(2,1)}, bf16[3,128,4,2,64]{1,4,3,2,0:...) while((s32[]{:T(128)}, f32[1536,4,64]{0,2,1:T(8,128)}, ...), condition=%wide.region_15.16_spmd.clone, body=%wide.region_13.15_spmd.clone.sunk | while | flops 1023474688 | bytes 98341240 | solution.py:277
  488.0 6.8 collective-permute-done.19
  496.1 7.8 collective-permute-done.20
  504.2 7.2 all_to_all.116
  514.6 7.2 all_to_all.117
  525.7 8.4 all_to_all.118
  540.1 6.7 convolution_convert_fusion.2
  546.9 6.5 convolution_convert_fusion.1
  554.4 6.6 convolution_convert_fusion
  562.4 14.0 %reduce-scatter.10.cloned.1.call-done = bf16[64,512]{1,0:T(8,128)(2,1)} async-done(((bf16[1024,512]{1,0:T(8,128)(2,1)}), bf16[64,512]{1,0:T(8,128)(2,1)}) %reduce-scatter.10.cloned.1.call-update) | async-done | bytes 65552 | tf_op jit(solution)/shard_map/reduce_scatter | solution.py:324
  576.4 60.5 %reduce-scatter.12.cloned.1.call-done = bf16[64,512]{1,0:T(8,128)(2,1)} async-done(((bf16[1024,512]{1,0:T(8,128)(2,1)}), bf16[64,512]{1,0:T(8,128)(2,1)}) %reduce-scatter.12.cloned.1.call-update) | async-done | bytes 65552 | tf_op jit(solution)/shard_map/reduce_scatter | solution.py:327
  636.9 64.3 %reduce-scatter.14.cloned.1.call-done = bf16[64,1024]{1,0:T(8,128)(2,1)} async-done(((bf16[1024,1024]{1,0:T(8,128)(2,1)}), bf16[64,1024]{1,0:T(8,128)(2,1)}) %reduce-scatter.14.cloned.1.call-update) | async-done | bytes 131088 | tf_op jit(solution)/shard_map/reduce_scatter | solution.py:336
  701.2 64.7 %reduce-scatter.8.cloned.1.call-done = bf16[64,1024]{1,0:T(8,128)(2,1)} async-done(((bf16[1024,1024]{1,0:T(8,128)(2,1)}), bf16[64,1024]{1,0:T(8,128)(2,1)}) %reduce-scatter.8.cloned.1.call-update) | async-done | bytes 131088 | tf_op jit(solution)/shard_map/reduce_scatter | solution.py:321
  765.9 114.5 %reduce-scatter.16.cloned.1.call-done = bf16[64,4608]{1,0:T(8,128)(2,1)} async-done(((bf16[1024,4608]{1,0:T(8,128)(2,1)}), bf16[64,4608]{1,0:T(8,128)(2,1)}) %reduce-scatter.16.cloned.1.call-update) | async-done | bytes 589840 | tf_op jit(solution)/shard_map/reduce_scatter | solution.py:342
  880.4 115.7 %reduce-scatter.18.cloned.1.call-done = bf16[64,4608]{1,0:T(8,128)(2,1)} async-done(((bf16[1024,4608]{1,0:T(8,128)(2,1)}), bf16[64,4608]{1,0:T(8,128)(2,1)}) %reduce-scatter.18.cloned.1.call-update) | async-done | bytes 589840 | tf_op jit(solution)/shard_map/reduce_scatter | solution.py:345
  996.0 115.2 %reduce-scatter.20.cloned.1.call-done = bf16[288,1024]{1,0:T(8,128)(2,1)} async-done(((bf16[4608,1024]{1,0:T(8,128)(2,1)}), bf16[288,1024]{1,0:T(8,128)(2,1)}) %reduce-scatter.20.cloned.1.call-update) | async-done | bytes 589840 | tf_op jit(solution)/shard_map/reduce_scatter | solution.py:348
  1111.3 7.1 fusion.48
  1120.7 32.6 %all-reduce.12 = (bf16[1024]{0:T(1024)(128)(2,1)S(1)}, bf16[64]{0:T(256)(128)(2,1)S(1)}, bf16[64]{0:T(256)(128)(2,1)S(1)}, bf16[1024]{0:T(1024)(128)(2,1)S(1)}) all-reduce(bf16[1024]{0:T(1024)(128)(2,1)S(1)} %get-tuple-element.276, bf16[64]{0:T(256)(128)(2,1)S(1)} %get-tuple-element.278, ...), channel_id=2, replica_groups=mesh['fsdp'=16,'seq'=2] {'fsdp'}, use_global_device_ids=true, to_apply=%region_20.21.clone | all-reduce | flops 2176 | bytes 8704
  1161.6 17.8 %all-reduce.18.cloned.1.call-done = (bf16[64,1024]{1,0:T(8,128)(2,1)}, bf16[64,512]{1,0:T(8,128)(2,1)}, bf16[64,512]{1,0:T(8,128)(2,1)}, bf16[64,1024]{1,0:T(8,1...) async-done(((bf16[64,1024]{1,0:T(8,128)(2,1)}, bf16[64,512]{1,0:T(8,128)(2,1)}, bf16[64,512]{1,0:T(8,128)(2,1)}, ...) | async-done | bytes 2162704 | tf_op jit(solution)/shard_map/psum | solution.py:354
  (453 shorter events, 251.6 us)
Async XLA Ops:
  7.2 70.9 %all-gather.9.cloned.1.call-start = ((), (), s32[]{:S(2)}) async-start(), calls=%async_computation.16 | async-start | bytes 1114112 | tf_op jit(solution)/shard_map/all_gather | solution.py:139
  7.9 89.5 %all-gather.11.cloned.1.call-start = ((), (), s32[]{:S(2)}) async-start(), calls=%async_computation.17 | async-start | bytes 1114112 | tf_op jit(solution)/shard_map/all_gather | solution.py:140
  8.7 162.9 %all-gather.7.cloned.1.call-start = ((), (), s32[]{:S(2)}) async-start(), calls=%async_computation.15 | async-start | bytes 2228224 | tf_op jit(solution)/shard_map/all_gather | solution.py:138
  9.4 210.6 %all-gather.13.cloned.1.call-start = ((), (), s32[]{:S(2)}) async-start(), calls=%async_computation.18 | async-start | bytes 2228224 | tf_op jit(solution)/shard_map/all_gather | solution.py:143
  10.0 280.6 %all-gather.15.cloned.1.call-start = ((), (), s32[]{:S(2)}) async-start(), calls=%async_computation.19 | async-start | bytes 10027008 | tf_op jit(solution)/shard_map/all_gather | solution.py:145
  10.6 361.7 %all-gather.17.cloned.1.call-start = ((), (), s32[]{:S(2)}) async-start(), calls=%async_computation.20 | async-start | bytes 10027008 | tf_op jit(solution)/shard_map/all_gather | solution.py:146
  10.6 14.6 %collective-permute-start.3 = (bf16[288,1024]{1,0:T(8,128)(2,1)}, bf16[288,1024]{1,0:T(8,128)(2,1)S(1)}, u32[]{:S(2)}, u32[]{:S(2)}) collective-permute-start(bf16[288,1024]{1,0:T(8,128)(2,1)} %param.31), channel_id=1, source_target_pairs={{0,2},{2,4},{4,6},{6,8},{8,10},{10,12},{12,14},{14,16},{16,18},{18... | collective-permute-start | bytes 1769480 | tf_op jit(solution)/shard_map/ppermute | solution.py:24
  11.1 16.8 %collective-permute-start.4 = (bf16[288,1024]{1,0:T(8,128)(2,1)}, bf16[288,1024]{1,0:T(8,128)(2,1)S(1)}, u32[]{:S(2)}, u32[]{:S(2)}) collective-permute-start(bf16[288,1024]{1,0:T(8,128)(2,1)} %param.31), channel_id=1, source_target_pairs={{0,30},{2,0},{4,2},{6,4},{8,6},{10,8},{12,10},{14,12},{16,14},{18,... | collective-permute-start | bytes 1769480 | tf_op jit(solution)/shard_map/ppermute | solution.py:27
  25.2 48.4 %collective-permute-start.5 = (bf16[288,1024]{1,0:T(8,128)(2,1)S(1)}, bf16[288,1024]{1,0:T(8,128)(2,1)S(1)}, u32[]{:S(2)}, u32[]{:S(2)}) collective-permute-start(bf16[288,1024]{1,0:T(8,128)(2,1)S(1)} %collective-permute-done.3), channel_id=1, source_target_pairs={{0,2},{2,4},{4,6},{6,8},{8,10},{10,12},{12,14},{14,16},{16,18},{18... | collective-permute-start | bytes 1769480 | tf_op jit(solution)/shard_map/ppermute | solution.py:24
  27.9 45.7 %collective-permute-start.6 = (bf16[288,1024]{1,0:T(8,128)(2,1)S(1)}, bf16[288,1024]{1,0:T(8,128)(2,1)}, u32[]{:S(2)}, u32[]{:S(2)}) collective-permute-start(bf16[288,1024]{1,0:T(8,128)(2,1)S(1)} %collective-permute-done.4), channel_id=1, source_target_pairs={{0,30},{2,0},{4,2},{6,4},{8,6},{10,8},{12,10},{14,12},{16,14},{18,... | collective-permute-start | bytes 1769480 | tf_op jit(solution)/shard_map/ppermute | solution.py:27
  73.6 30.5 %collective-permute-start.7 = (bf16[288,1024]{1,0:T(8,128)(2,1)S(1)}, bf16[288,1024]{1,0:T(8,128)(2,1)}, u32[]{:S(2)}, u32[]{:S(2)}) collective-permute-start(bf16[288,1024]{1,0:T(8,128)(2,1)S(1)} %collective-permute-done.5), channel_id=1, source_target_pairs={{0,2},{2,4},{4,6},{6,8},{8,10},{10,12},{12,14},{14,16},{16,18},{18... | collective-permute-start | bytes 1769480 | tf_op jit(solution)/shard_map/ppermute | solution.py:24
  73.6 30.7 %collective-permute-start.8 = (bf16[288,1024]{1,0:T(8,128)(2,1)}, bf16[288,1024]{1,0:T(8,128)(2,1)}, u32[]{:S(2)}, u32[]{:S(2)}) collective-permute-start(bf16[288,1024]{1,0:T(8,128)(2,1)} %collective-permute-done.6), channel_id=1, source_target_pairs={{0,30},{2,0},{4,2},{6,4},{8,6},{10,8},{12,10},{14,12},{16,14},{18,... | collective-permute-start | bytes 1769480 | tf_op jit(solution)/shard_map/ppermute | solution.py:27
  81.7 18.1 %all-to-all-start.1 = ((bf16[192,2,256]{2,0,1:T(8,128)(2,1)}), bf16[192,2,256]{2,0,1:T(8,128)(2,1)S(1)}, u32[]{:S(2)}, u32[]{:S(2)}) async-start(bf16[192,2,256]{2,0,1:T(8,128)(2,1)} %copy.117), calls=%async_computation.1 | async-start | bytes 393216 | tf_op jit(solution)/shard_map/all_to_all | solution.py:179
  104.1 14.5 %collective-permute-start.9 = (bf16[288,1024]{1,0:T(8,128)(2,1)}, bf16[288,1024]{1,0:T(8,128)(2,1)}, u32[]{:S(2)}, u32[]{:S(2)}) collective-permute-start(bf16[288,1024]{1,0:T(8,128)(2,1)} %collective-permute-done.7), channel_id=1, source_target_pairs={{0,2},{2,4},{4,6},{6,8},{8,10},{10,12},{12,14},{14,16},{16,18},{18... | collective-permute-start | bytes 1769480 | tf_op jit(solution)/shard_map/ppermute | solution.py:24
  104.3 17.4 %collective-permute-start.10 = (bf16[288,1024]{1,0:T(8,128)(2,1)}, bf16[288,1024]{1,0:T(8,128)(2,1)}, u32[]{:S(2)}, u32[]{:S(2)}) collective-permute-start(bf16[288,1024]{1,0:T(8,128)(2,1)} %collective-permute-done.8), channel_id=1, source_target_pairs={{0,30},{2,0},{4,2},{6,4},{8,6},{10,8},{12,10},{14,12},{16,14},{18,... | collective-permute-start | bytes 1769480 | tf_op jit(solution)/shard_map/ppermute | solution.py:27
  108.6 14.4 %collective-permute-start = (bf16[2,384,256]{2,1,0:T(8,128)(2,1)S(1)}, bf16[2,384,256]{2,1,0:T(8,128)(2,1)S(1)}, u32[]{:S(2)}, u32[]{:S(2)}) collective-permute-start(bf16[2,384,256]{2,1,0:T(8,128)(2,1)S(1)} %pad_maximum_fusion.3), channel_id=1, source_target_pairs={{0,2},{2,4},{4,6},{6,8},{8,10},{10,12},{12,14},{14,16},{16,18},{18... | collective-permute-start | bytes 1179656 | tf_op jit(solution)/shard_map/ppermute | solution.py:37
  118.5 32.1 %collective-permute-start.11 = (bf16[288,1024]{1,0:T(8,128)(2,1)}, bf16[288,1024]{1,0:T(8,128)(2,1)}, u32[]{:S(2)}, u32[]{:S(2)}) collective-permute-start(bf16[288,1024]{1,0:T(8,128)(2,1)} %collective-permute-done.9), channel_id=1, source_target_pairs={{0,2},{2,4},{4,6},{6,8},{8,10},{10,12},{12,14},{14,16},{16,18},{18... | collective-permute-start | bytes 1769480 | tf_op jit(solution)/shard_map/ppermute | solution.py:24
  121.8 31.4 %collective-permute-start.12 = (bf16[288,1024]{1,0:T(8,128)(2,1)}, bf16[288,1024]{1,0:T(8,128)(2,1)}, u32[]{:S(2)}, u32[]{:S(2)}) collective-permute-start(bf16[288,1024]{1,0:T(8,128)(2,1)} %collective-permute-done.10), channel_id=1, source_target_pairs={{0,30},{2,0},{4,2},{6,4},{8,6},{10,8},{12,10},{14,12},{16,14},{18,... | collective-permute-start | bytes 1769480 | tf_op jit(solution)/shard_map/ppermute | solution.py:27
  123.0 15.4 %collective-permute-start.1 = (bf16[2,384,256]{2,1,0:T(8,128)(2,1)S(1)}, bf16[2,384,256]{2,1,0:T(8,128)(2,1)S(1)}, u32[]{:S(2)}, u32[]{:S(2)}) collective-permute-start(bf16[2,384,256]{2,1,0:T(8,128)(2,1)S(1)} %collective-permute-done), channel_id=1, source_target_pairs={{0,2},{2,4},{4,6},{6,8},{8,10},{10,12},{12,14},{14,16},{16,18},{18... | collective-permute-start | bytes 1179656 | tf_op jit(solution)/shard_map/ppermute | solution.py:37
  138.4 20.7 %collective-permute-start.2 = (bf16[2,384,256]{2,1,0:T(8,128)(2,1)S(1)}, bf16[2,384,256]{2,1,0:T(8,128)(2,1)S(1)}, u32[]{:S(2)}, u32[]{:S(2)}) collective-permute-start(bf16[2,384,256]{2,1,0:T(8,128)(2,1)S(1)} %collective-permute-done.1), channel_id=1, source_target_pairs={{0,2},{2,4},{4,6},{6,8},{8,10},{10,12},{12,14},{14,16},{16,18},{18... | collective-permute-start | bytes 1179656 | tf_op jit(solution)/shard_map/ppermute | solution.py:37
  153.2 18.4 %collective-permute-start.14 = (bf16[288,1024]{1,0:T(8,128)(2,1)}, bf16[288,1024]{1,0:T(8,128)(2,1)}, u32[]{:S(2)}, u32[]{:S(2)}) collective-permute-start(bf16[288,1024]{1,0:T(8,128)(2,1)} %collective-permute-done.12), channel_id=1, source_target_pairs={{0,30},{2,0},{4,2},{6,4},{8,6},{10,8},{12,10},{14,12},{16,14},{18,... | collective-permute-start | bytes 1769480 | tf_op jit(solution)/shard_map/ppermute | solution.py:27
  163.1 20.9 %collective-permute-start.15 = (bf16[288,1024]{1,0:T(8,128)(2,1)}, bf16[288,1024]{1,0:T(8,128)(2,1)}, u32[]{:S(2)}, u32[]{:S(2)}) collective-permute-start(bf16[288,1024]{1,0:T(8,128)(2,1)} %collective-permute-done.13), channel_id=1, source_target_pairs={{0,2},{2,4},{4,6},{6,8},{8,10},{10,12},{12,14},{14,16},{16,18},{18... | collective-permute-start | bytes 1769480 | tf_op jit(solution)/shard_map/ppermute | solution.py:24
  171.6 43.4 %collective-permute-start.16 = (bf16[288,1024]{1,0:T(8,128)(2,1)}, bf16[288,1024]{1,0:T(8,128)(2,1)}, u32[]{:S(2)}, u32[]{:S(2)}) collective-permute-start(bf16[288,1024]{1,0:T(8,128)(2,1)} %collective-permute-done.14), channel_id=1, source_target_pairs={{0,30},{2,0},{4,2},{6,4},{8,6},{10,8},{12,10},{14,12},{16,14},{18,... | collective-permute-start | bytes 1769480 | tf_op jit(solution)/shard_map/ppermute | solution.py:27
  184.0 39.9 %collective-permute-start.17 = (bf16[288,1024]{1,0:T(8,128)(2,1)}, bf16[288,1024]{1,0:T(8,128)(2,1)}, u32[]{:S(2)}, u32[]{:S(2)}) collective-permute-start(bf16[288,1024]{1,0:T(8,128)(2,1)} %collective-permute-done.15), channel_id=1, source_target_pairs={{0,2},{2,4},{4,6},{6,8},{8,10},{10,12},{12,14},{14,16},{16,18},{18... | collective-permute-start | bytes 1769480 | tf_op jit(solution)/shard_map/ppermute | solution.py:24
  409.3 167.2 %reduce-scatter.10.cloned.1.call-start = ((), (), s32[]{:S(2)}) async-start(), calls=%async_computation.22 | async-start | bytes 1114112 | tf_op jit(solution)/shard_map/reduce_scatter | solution.py:324
  514.4 122.5 %reduce-scatter.12.cloned.1.call-start = ((), (), s32[]{:S(2)}) async-start(), calls=%async_computation.23 | async-start | bytes 1114112 | tf_op jit(solution)/shard_map/reduce_scatter | solution.py:327
  523.5 177.7 %reduce-scatter.14.cloned.1.call-start = ((), (), s32[]{:S(2)}) async-start(), calls=%async_computation.24 | async-start | bytes 2228224 | tf_op jit(solution)/shard_map/reduce_scatter | solution.py:336
  525.7 240.2 %reduce-scatter.8.cloned.1.call-start = ((), (), s32[]{:S(2)}) async-start(), calls=%async_computation.21 | async-start | bytes 2228224 | tf_op jit(solution)/shard_map/reduce_scatter | solution.py:321
  539.9 340.5 %reduce-scatter.16.cloned.1.call-start = ((), (), s32[]{:S(2)}) async-start(), calls=%async_computation.25 | async-start | bytes 10027008 | tf_op jit(solution)/shard_map/reduce_scatter | solution.py:342
  546.8 449.2 %reduce-scatter.18.cloned.1.call-start = ((), (), s32[]{:S(2)}) async-start(), calls=%async_computation.26 | async-start | bytes 10027008 | tf_op jit(solution)/shard_map/reduce_scatter | solution.py:345
  553.4 557.8 %reduce-scatter.20.cloned.1.call-start = ((), (), s32[]{:S(2)}) async-start(), calls=%async_computation.27 | async-start | bytes 10027008 | tf_op jit(solution)/shard_map/reduce_scatter | solution.py:348
  561.0 618.4 %all-reduce.18.cloned.1.call-start = ((), (), s32[]{:S(2)}) async-start(), calls=%async_computation.28 | async-start | bytes 4325376 | tf_op jit(solution)/shard_map/psum | solution.py:354
  (96 other events, 2303.5 us)
Sparse Core Ops, SparseCore 0:
  10.2 46.6 all-gather.8
  59.0 38.3 all-gather.10
  99.6 57.5 all-gather.6
  159.2 49.3 all-gather.12
  210.7 79.7 all-gather.14
  292.7 79.5 all-gather.16
  514.6 61.8 reduce-scatter.9
  580.5 56.3 reduce-scatter.11
  640.7 60.4 reduce-scatter.13
  705.3 60.5 reduce-scatter.7
  770.0 110.3 reduce-scatter.15
  884.9 111.1 reduce-scatter.17
  1000.1 111.0 reduce-scatter.19
  1114.1 65.2 all-reduce.17
